TPU v7x, 256 devices: a whole 4x4x8 slice. The times are simulated.
256 devices in a mesh: azim: 64 (over x, y_hi, z), axial: 4 (over y_lo, core).
Axes of the slice: x: 4, y: 4 (y_hi: 2, y_lo: 2; y = y_hi * 2 + y_lo), z: 8, core: 2. Of those that a mesh axis runs over, the one named last changes fastest.
Arguments:
- rhs: float32 [64, 48, 4, 128], P('azim', None, 'axial'), may hold values from -6 to 6
- coupling: float32 [64, 48, 4, 128], P('azim', None, 'axial'), may hold values from 0.2 to 0.5
- fwd_coupling: bfloat16 [64, 48, 48, 4, 128], P('azim', None, None, 'axial'), may hold values from -1 to 1
- bwd_coupling: bfloat16 [64, 48, 48, 4, 128], P('azim', None, None, 'axial'), may hold values from -1 to 1
- block_inverse: bfloat16 [64, 48, 48, 4, 128], P('azim', None, None, 'axial'), may hold values from -1 to 1
Outputs:
- correction: float32 [64, 48, 4, 128], P('azim', None, 'axial')
- remaining: float32 [64, 48, 4, 128], P('azim', None, 'axial')
All inputs are finite; a program needn't handle non-finite values.
Results may differ from a plain program's by a relative error of at most 0.0003.
Values sent between devices are 32-bit elements; how exact they have to be, the bound alone decides.
A program may use at most 128 MiB of HBM per device.

v0:
```python
import jax
import jax.numpy as jnp
from jax import lax
from jax.sharding import PartitionSpec as P

highest = lax.Precision.HIGHEST


def from_behind(value, axis, steps):
    count = lax.axis_size(axis)
    initial, last = (max(0, -steps), min(count, count - steps))
    return lax.ppermute(value, axis, [(source, source + steps) for source in range(initial, last)])


def from_root(shard, axis, root):
    mine = lax.axis_index(axis) == root
    return lax.psum(jnp.where(mine, shard, jnp.zeros_like(shard)), axis)


def extended(block, sides, width):
    for axis, dim in sides:
        count = lax.axis_size(axis)
        forward = [(i, i + 1) for i in range(count - 1)]
        backward = [(target, source) for source, target in forward]
        low = lax.ppermute(
            lax.slice_in_dim(block, block.shape[dim] - width, None, axis=dim), axis, forward
        )
        high = lax.ppermute(lax.slice_in_dim(block, 0, width, axis=dim), axis, backward)
        block = jnp.concatenate([low, block, high], axis=dim)
    return block


def cell_stride(one_block, carried, const_term):
    return const_term - jnp.einsum(
        "abl,al->bl", one_block.astype(jnp.float32), carried, precision=highest
    )


def compose_cells(blocks, sequence):
    running = None
    for position in sequence:
        one_block = blocks[position].astype(jnp.float32)
        running = -jnp.swapaxes(one_block, 0, 1)
    return running


def doubling_maps(local_map, reverse):
    size = lax.axis_size("azim")
    index = lax.axis_index("azim")
    levels = []
    current = local_map
    distance = 1
    while distance < size:
        if reverse:
            moved = from_behind(current, "azim", -distance)
            exists = index + distance < size
        else:
            moved = from_behind(current, "azim", distance)
            exists = index >= distance
        levels.append((current, distance))
        current = jnp.where(
            exists, jnp.einsum("bcl,cal->bal", current, moved, precision=highest), current
        )
        distance = distance * 2
    return (levels, current)


def doubling_entries(map_levels, local_offset, reverse):
    levels, final_map = map_levels
    size = lax.axis_size("azim")
    index = lax.axis_index("azim")
    running = local_offset
    for current, distance in levels:
        if reverse:
            moved = from_behind(running, "azim", -distance)
        else:
            moved = from_behind(running, "azim", distance)
        running = jnp.einsum("bcl,cl->bl", current, moved, precision=highest) + running
    if reverse:
        wrapped = from_root(running, "azim", 0)
    else:
        wrapped = from_root(running, "azim", size - 1)
    leaving = jnp.einsum("bcl,cl->bl", final_map, wrapped, precision=highest) + running
    if reverse:
        shifted = from_behind(leaving, "azim", -1)
        first_device = index == size - 1
    else:
        shifted = from_behind(leaving, "azim", 1)
        first_device = index == 0
    return jnp.where(first_device, wrapped, shifted)


def sweep(blocks, consts, map_levels, reverse):
    cell_count = blocks.shape[0]
    sequence = list(range(cell_count))
    if reverse:
        sequence = sequence[::-1]
    carried = jnp.zeros(consts.shape[1:], jnp.float32)
    for position in sequence:
        carried = cell_stride(blocks[position], carried, consts[position])
    local_offset = carried
    incoming_maps = doubling_entries(map_levels, local_offset, reverse)
    outputs = [None] * cell_count
    carried = incoming_maps
    for position in sequence:
        carried = cell_stride(blocks[position], carried, consts[position])
        outputs[position] = carried
    return jnp.stack(outputs)


def on_device(rhs, coupling, fwd_coupling, bwd_coupling, block_inverse):
    cell_count, block_width, _, position_total, radial_count = fwd_coupling.shape
    line_count = position_total * radial_count
    forward_blocks = fwd_coupling.reshape(cell_count, block_width, block_width, line_count)
    backward_blocks = bwd_coupling.reshape(cell_count, block_width, block_width, line_count)
    inverse_blocks = block_inverse.reshape(cell_count, block_width, block_width, line_count)
    source = rhs.reshape(cell_count, block_width, line_count)
    coupling_field = coupling.reshape(cell_count, block_width, line_count)
    forward_map = compose_cells(forward_blocks, list(range(cell_count)))
    backward_map = compose_cells(backward_blocks, list(range(cell_count))[::-1])
    forward_levels = None
    backward_levels = None
    forward_levels = doubling_maps(forward_map, False)
    backward_levels = doubling_maps(backward_map, True)

    def precondition(vector):
        consts = jnp.stack(
            [
                jnp.einsum(
                    "abl,al->bl",
                    inverse_blocks[0].astype(jnp.float32),
                    vector[0],
                    precision=highest,
                )
            ]
        )
        forward = sweep(forward_blocks, consts, forward_levels, False)
        return sweep(backward_blocks, forward, backward_levels, True)

    def stations_sum(field):
        grid = field.reshape(cell_count, block_width, position_total, radial_count)
        padded = extended(grid, (("axial", 2),), 1)
        return (padded[:, :, :-2] + padded[:, :, 2:]).reshape(cell_count, block_width, line_count)

    applied_once = precondition(source)
    middle = source - applied_once + coupling_field * stations_sum(applied_once)
    second = precondition(middle)
    correction = applied_once + second
    remaining = middle - second + coupling_field * stations_sum(second)
    return (correction.reshape(rhs.shape), remaining.reshape(rhs.shape))


def solution(mesh):
    return jax.shard_map(
        on_device,
        mesh=mesh,
        in_specs=(
            P("azim", None, "axial", None),
            P("azim", None, "axial", None),
            P("azim", None, None, "axial", None),
            P("azim", None, None, "axial", None),
            P("azim", None, None, "axial", None),
        ),
        out_specs=(P("azim", None, "axial", None), P("azim", None, "axial", None)),
        check_vma=False,
    )
```

profile of v0, /device:TPU:1, one launch (start us, length us, event | category | flops | bytes accessed | tf_op | source)
XLA Modules:
  0.0 2142.2 jit_solution(16091125914390163233)
XLA Ops:
  7.7 5.4 collective-permute-start.2
  19.5 17.9 collective-permute-done
  38.6 5.6 collective-permute-start.1
  48.5 7.0 multiply_reduce_fusion.26
  57.5 8.3 collective-permute-start.4
  65.9 5.0 collective-permute-start.3
  71.0 42.8 %collective-permute-done.3 = f32[48,128]{1,0:T(8,128)S(1)} collective-permute-done((f32[48,128]{1,0:T(8,128)S(1)}, f32[48,128]{1,0:T(8,128)S(1)}, u32[]{:S(2)}, u32[]{:S(2)}) %collective-permute-start.3) | collective-permute-done | bytes 24608 | tf_op jit(solution)/shard_map/ppermute | solution.py:12
  117.1 6.5 multiply_reduce_fusion.25
  126.8 9.3 collective-permute-start.6
  136.2 6.0 collective-permute-start.5
  143.2 17.2 collective-permute-done.6
  163.7 9.3 multiply_reduce_fusion.24
  176.3 38.1 %collective-permute-start.8 = (f32[48,48,128]{2,1,0:T(8,128)}, f32[48,48,128]{2,1,0:T(8,128)}, u32[]{:S(2)}, u32[]{:S(2)}) collective-permute-start(f32[48,48,128]{2,1,0:T(8,128)} %copy.30), channel_id=1, source_target_pairs={{0,32},{4,36},{8,40},{12,44},{16,48},{20,52},{24,56},{28,60},{32,6... | collective-permute-start | bytes 3538952 | tf_op jit(solution)/shard_map/ppermute | solution.py:12
  218.1 17.8 collective-permute-done.8
  239.2 9.4 multiply_reduce_fusion.23
  251.8 9.1 collective-permute-start.10
  261.0 3.8 collective-permute-start.9
  264.9 16.8 collective-permute-done.9
  285.1 9.3 multiply_reduce_fusion.22
  297.6 6.4 collective-permute-start.11
  317.1 319.2 %psum.28 = f32[48,128]{1,0:T(8,128)S(1)} all-reduce(f32[48,128]{1,0:T(8,128)S(1)} %broadcast_select_fusion.2), channel_id=1, replica_groups=mesh['azim'=64,'axial'=4] {'azim'}, use_global_device_ids=true, to_apply=%region_0.1 | all-reduce | flops 6144 | bytes 49152 | tf_op jit(solution)/shard_map/psum | solution.py:17
  639.8 9.3 multiply_reduce_fusion.21
  668.1 8.6 multiply_reduce_fusion.19
  682.8 7.7 collective-permute-done.16
  690.6 19.6 collective-permute-done.17
  713.5 9.3 multiply_reduce_fusion.18
  728.7 5.9 collective-permute-done.18
  734.7 12.6 collective-permute-done.19
  750.6 9.5 multiply_reduce_fusion.17
  766.2 12.0 collective-permute-done.20
  778.4 3.7 collective-permute-done.21
  785.4 9.4 multiply_reduce_fusion.16
  800.7 5.2 collective-permute-done.22
  805.9 9.6 collective-permute-done.23
  818.8 9.5 multiply_reduce_fusion.15
  832.8 343.0 %psum.29 = f32[48,128]{1,0:T(8,128)S(1)} all-reduce(f32[48,128]{1,0:T(8,128)S(1)} %broadcast_select_fusion), channel_id=1, replica_groups=mesh['azim'=64,'axial'=4] {'azim'}, use_global_device_ids=true, to_apply=%region_1.2 | all-reduce | flops 6144 | bytes 49152 | tf_op jit(solution)/shard_map/psum | solution.py:17
  1179.3 9.3 multiply_reduce_fusion.14
  1195.8 108.7 %collective-permute-start.27 = (f32[1,48,1,128]{3,1,2,0:T(8,128)S(1)}, f32[1,48,1,128]{3,1,2,0:T(8,128)S(1)}, u32[]{:S(2)}, u32[]{:S(2)}) collective-permute-start(f32[1,48,1,128]{3,1,2,0:T(8,128)S(1)} %subtract_bitcast_fusion.5), channel_id=1, source_target_pairs={{1,0},{2,1},{3,2},{5,4},{6,5},{7,6},{9,8},{10,9},{11,10},{13,12},{... | collective-permute-start | bytes 73736 | tf_op jit(solution)/shard_map/ppermute | solution.py:28
  1319.0 5.7 collective-permute-start.30
  1328.2 4.9 collective-permute-start.31
  1342.4 4.0 collective-permute-start.33
  1348.5 300.0 %psum.30 = f32[48,128]{1,0:T(8,128)S(1)} all-reduce(f32[48,128]{1,0:T(8,128)S(1)} %broadcast_select_fusion.1), channel_id=1, replica_groups=mesh['azim'=64,'axial'=4] {'azim'}, use_global_device_ids=true, to_apply=%region_2.3 | all-reduce | flops 6144 | bytes 49152 | tf_op jit(solution)/shard_map/psum | solution.py:17
  1664.4 4.0 collective-permute-done.36
  1671.2 7.5 collective-permute-done.37
  1682.6 5.1 collective-permute-done.38
  1697.7 4.8 collective-permute-done.40
  1703.7 296.5 %psum.31 = f32[48,128]{1,0:T(8,128)S(1)} all-reduce(f32[48,128]{1,0:T(8,128)S(1)} %broadcast_select_fusion.3), channel_id=1, replica_groups=mesh['azim'=64,'axial'=4] {'azim'}, use_global_device_ids=true, to_apply=%region_3.4 | all-reduce | flops 6144 | bytes 49152 | tf_op jit(solution)/shard_map/psum | solution.py:17
  2008.5 128.7 %collective-permute-start.43 = (f32[1,48,1,128]{3,1,2,0:T(8,128)S(1)}, f32[1,48,1,128]{3,1,2,0:T(8,128)S(1)}, u32[]{:S(2)}, u32[]{:S(2)}) collective-permute-start(f32[1,48,1,128]{3,1,2,0:T(8,128)S(1)} %subtract_bitcast_fusion.4), channel_id=1, source_target_pairs={{1,0},{2,1},{3,2},{5,4},{6,5},{7,6},{9,8},{10,9},{11,10},{13,12},{... | collective-permute-start | bytes 73736 | tf_op jit(solution)/shard_map/ppermute | solution.py:28
  (236 shorter events, 215.7 us)
Async XLA Ops:
  2.5 35.1 %copy-start.5 = (bf16[1,48,48,1,128]{2,1,4,3,0:T(8,128)(2,1)}, bf16[1,48,48,1,128]{2,1,4,3,0:T(8,128)(2,1)S(1)}, u32[]{:S(2)}) copy-start(bf16[1,48,48,1,128]{2,1,4,3,0:T(8,128)(2,1)S(1)} %copy.21) | copy-start | bytes 1769476
  7.7 37.5 %collective-permute-start.2 = (f32[48,48,128]{2,1,0:T(8,128)}, f32[48,48,128]{2,1,0:T(8,128)}, u32[]{:S(2)}, u32[]{:S(2)}) collective-permute-start(f32[48,48,128]{2,1,0:T(8,128)} %copy.22), channel_id=1, source_target_pairs={{0,4},{4,8},{8,12},{12,16},{16,20},{20,24},{24,28},{28,32},{32,36}... | collective-permute-start | bytes 3538952 | tf_op jit(solution)/shard_map/ppermute | solution.py:12
  15.0 30.3 %copy-start.6 = (bf16[128,48,48]{2,1,0:T(8,128)(2,1)}, bf16[128,48,48]{2,1,0:T(8,128)(2,1)S(1)}, u32[]{:S(2)}) copy-start(bf16[128,48,48]{2,1,0:T(8,128)(2,1)S(1)} %copy.68) | copy-start | bytes 1769476
  17.0 20.5 collective-permute-start
  38.6 6.5 collective-permute-start.1
  57.5 56.3 %collective-permute-start.4 = (f32[48,48,128]{2,1,0:T(8,128)}, f32[48,48,128]{2,1,0:T(8,128)}, u32[]{:S(2)}, u32[]{:S(2)}) collective-permute-start(f32[48,48,128]{2,1,0:T(8,128)} %copy.24), channel_id=1, source_target_pairs={{0,8},{4,12},{8,16},{12,20},{16,24},{20,28},{24,32},{28,36},{32,40... | collective-permute-start | bytes 3538952 | tf_op jit(solution)/shard_map/ppermute | solution.py:12
  65.9 47.8 %collective-permute-start.3 = (f32[48,128]{1,0:T(8,128)S(1)}, f32[48,128]{1,0:T(8,128)S(1)}, u32[]{:S(2)}, u32[]{:S(2)}) collective-permute-start(f32[48,128]{1,0:T(8,128)S(1)} %bitcast_add_fusion.29), channel_id=1, source_target_pairs={{0,16},{4,20},{8,24},{12,28},{16,32},{20,36},{24,40},{28,44},{32,4... | collective-permute-start | bytes 73736 | tf_op jit(solution)/shard_map/ppermute | solution.py:12
  126.8 33.5 %collective-permute-start.6 = (f32[48,48,128]{2,1,0:T(8,128)}, f32[48,48,128]{2,1,0:T(8,128)}, u32[]{:S(2)}, u32[]{:S(2)}) collective-permute-start(f32[48,48,128]{2,1,0:T(8,128)} %copy.27), channel_id=1, source_target_pairs={{0,16},{4,20},{8,24},{12,28},{16,32},{20,36},{24,40},{28,44},{32,4... | collective-permute-start | bytes 3538952 | tf_op jit(solution)/shard_map/ppermute | solution.py:12
  136.2 6.9 collective-permute-start.5
  176.3 59.7 %collective-permute-start.8 = (f32[48,48,128]{2,1,0:T(8,128)}, f32[48,48,128]{2,1,0:T(8,128)}, u32[]{:S(2)}, u32[]{:S(2)}) collective-permute-start(f32[48,48,128]{2,1,0:T(8,128)} %copy.30), channel_id=1, source_target_pairs={{0,32},{4,36},{8,40},{12,44},{16,48},{20,52},{24,56},{28,60},{32,6... | collective-permute-start | bytes 3538952 | tf_op jit(solution)/shard_map/ppermute | solution.py:12
  214.5 3.5 collective-permute-start.7
  251.8 30.0 %collective-permute-start.10 = (f32[48,48,128]{2,1,0:T(8,128)}, f32[48,48,128]{2,1,0:T(8,128)}, u32[]{:S(2)}, u32[]{:S(2)}) collective-permute-start(f32[48,48,128]{2,1,0:T(8,128)} %copy.33), channel_id=1, source_target_pairs={{0,64},{4,68},{8,72},{12,76},{16,80},{20,84},{24,88},{28,92},{32,9... | collective-permute-start | bytes 3538952 | tf_op jit(solution)/shard_map/ppermute | solution.py:12
  261.0 20.6 collective-permute-start.9
  297.6 338.9 %collective-permute-start.11 = (f32[48,48,128]{2,1,0:T(8,128)}, f32[48,48,128]{2,1,0:T(8,128)}, u32[]{:S(2)}, u32[]{:S(2)}) collective-permute-start(f32[48,48,128]{2,1,0:T(8,128)} %copy.36), channel_id=1, source_target_pairs={{0,128},{4,132},{8,136},{12,140},{16,144},{20,148},{24,152},{28,15... | collective-permute-start | bytes 3538952 | tf_op jit(solution)/shard_map/ppermute | solution.py:12
  313.1 350.7 %collective-permute-start.15 = (f32[48,48,128]{2,1,0:T(8,128)}, f32[48,48,128]{2,1,0:T(8,128)}, u32[]{:S(2)}, u32[]{:S(2)}) collective-permute-start(f32[48,48,128]{2,1,0:T(8,128)} %copy.40), channel_id=1, source_target_pairs={{4,0},{8,4},{12,8},{16,12},{20,16},{24,20},{28,24},{32,28},{36,32}... | collective-permute-start | bytes 3538952 | tf_op jit(solution)/shard_map/ppermute | solution.py:12
  649.2 3.8 collective-permute-start.12
  655.3 4.9 collective-permute-start.13
  662.5 5.5 collective-permute-start.14
  680.0 30.3 %collective-permute-start.17 = (f32[48,48,128]{2,1,0:T(8,128)}, f32[48,48,128]{2,1,0:T(8,128)}, u32[]{:S(2)}, u32[]{:S(2)}) collective-permute-start(f32[48,48,128]{2,1,0:T(8,128)} %copy.42), channel_id=1, source_target_pairs={{8,0},{12,4},{16,8},{20,12},{24,16},{28,20},{32,24},{36,28},{40,32... | collective-permute-start | bytes 3538952 | tf_op jit(solution)/shard_map/ppermute | solution.py:12
  681.3 9.2 collective-permute-start.16
  726.1 21.3 collective-permute-start.19
  727.4 7.2 collective-permute-start.18
  763.3 18.8 collective-permute-start.21
  764.7 13.6 collective-permute-start.20
  798.0 17.5 collective-permute-start.23
  799.4 6.5 collective-permute-start.22
  831.5 344.5 %collective-permute-start.24 = (f32[48,48,128]{2,1,0:T(8,128)}, f32[48,48,128]{2,1,0:T(8,128)}, u32[]{:S(2)}, u32[]{:S(2)}) collective-permute-start(f32[48,48,128]{2,1,0:T(8,128)} %copy.54), channel_id=1, source_target_pairs={{128,0},{132,4},{136,8},{140,12},{144,16},{148,20},{152,24},{156,2... | collective-permute-start | bytes 3538952 | tf_op jit(solution)/shard_map/ppermute | solution.py:12
  1179.3 128.4 %copy-start.9 = (f32[1,48,1,128]{3,2,1,0:T(1,128)S(1)}, f32[1,48,1,128]{3,2,1,0:T(1,128)}, u32[]{:S(2)}) copy-start(f32[1,48,1,128]{3,2,1,0:T(1,128)} %param.6) | copy-start | bytes 73732
  1188.6 4.9 collective-permute-start.25
  1195.8 110.7 %collective-permute-start.27 = (f32[1,48,1,128]{3,1,2,0:T(8,128)S(1)}, f32[1,48,1,128]{3,1,2,0:T(8,128)S(1)}, u32[]{:S(2)}, u32[]{:S(2)}) collective-permute-start(f32[1,48,1,128]{3,1,2,0:T(8,128)S(1)} %subtract_bitcast_fusion.5), channel_id=1, source_target_pairs={{1,0},{2,1},{3,2},{5,4},{6,5},{7,6},{9,8},{10,9},{11,10},{13,12},{... | collective-permute-start | bytes 73736 | tf_op jit(solution)/shard_map/ppermute | solution.py:28
  1304.6 3.1 collective-permute-start.26
  1308.9 2.3 collective-permute-start.28
  1313.5 4.3 collective-permute-start.29
  1319.0 6.7 collective-permute-start.30
  1328.2 5.8 collective-permute-start.31
  1335.2 4.6 collective-permute-start.32
  1342.4 4.9 collective-permute-start.33
  1651.2 2.2 collective-permute-start.34
  1655.8 4.8 collective-permute-start.35
  1663.0 5.5 collective-permute-start.36
  1669.6 9.0 collective-permute-start.37
  1681.3 6.4 collective-permute-start.38
  1688.8 5.0 collective-permute-start.39
  1696.4 6.1 collective-permute-start.40
  1703.6 303.9 %copy-start.7 = (bf16[128,48,48]{2,1,0:T(8,128)(2,1)S(1)}, bf16[128,48,48]{2,1,0:T(8,128)(2,1)}, u32[]{:S(2)}) copy-start(bf16[128,48,48]{2,1,0:T(8,128)(2,1)} %copy.127) | copy-start | bytes 1769476
  2002.8 4.6 collective-permute-start.41
  2008.5 131.9 %collective-permute-start.43 = (f32[1,48,1,128]{3,1,2,0:T(8,128)S(1)}, f32[1,48,1,128]{3,1,2,0:T(8,128)S(1)}, u32[]{:S(2)}, u32[]{:S(2)}) collective-permute-start(f32[1,48,1,128]{3,1,2,0:T(8,128)S(1)} %subtract_bitcast_fusion.4), channel_id=1, source_target_pairs={{1,0},{2,1},{3,2},{5,4},{6,5},{7,6},{9,8},{10,9},{11,10},{13,12},{... | collective-permute-start | bytes 73736 | tf_op jit(solution)/shard_map/ppermute | solution.py:28
  2137.3 4.1 collective-permute-start.42
  (6 other events, 90.7 us)
where the time goes:
time: 2150 us; the launch traced here: 2140 us
  blocking collectives  1260 us (59%)
  starting transfers between devices  397 us (18%)
  waiting for transfers between devices  240 us (11%)
  matrix products  106 us (5%)
  local copies, waits for them, and re-layouts  90.9 us (4%)
  other arithmetic  47 us (2%)
    psum x4, blocking collectives, from_root(): return lax.psum(jnp.where(mine, shard, jnp.zeros_like(shard)), axis)  1260 us
    ppermute x40, waiting for transfers between devices, from_behind(): lax.ppermute(value, axis, [(source, source + steps) for source in range(i...  238 us
    ppermute x2, starting transfers between devices, extended(): lax.ppermute(lax.slice_in_dim(block, 0, width, axis=dim), axis, backward)  237 us
    ppermute x40, starting transfers between devices, from_behind(): lax.ppermute(value, axis, [(source, source + steps) for source in range(i...  155 us
    dot_general x12, matrix products, doubling_maps(): jnp.einsum('bcl,cal->bal', current, moved, precision=highest)  106 us
  transfers between devices with their start and end apart: 44, of which 35 were waited for; matrix products, arithmetic and copies ran while one was open for 2% of the time, Pallas kernels for 0%

commit v1 on v0

--- a/solution.py
+++ b/solution.py
@@ -14,7 +14,7 @@
 
 def from_root(shard, axis, root):
     mine = lax.axis_index(axis) == root
-    return lax.psum(jnp.where(mine, shard, jnp.zeros_like(shard)), axis)
+    return jnp.sum(lax.all_gather(jnp.where(mine, shard, jnp.zeros_like(shard)), axis), axis=0)
 
 
 def extended(block, sides, width):

time: 2150 us -> 1260 us (0.59)
  blocking collectives: 1260 us -> 0 us
  waiting for transfers between devices: 240 us -> 788 us
  starting transfers between devices: 397 us -> 198 us
    psum x4 -> x0, blocking collectives: 1260 us -> none  [from_root(): return lax.psum(jnp.where(mine, shard, jnp.zeros_like(shard)), axis)]
    all_gather x0 -> x4, waiting for transfers between devices: none -> 492 us  [from_root(): lax.all_gather(jnp.where(mine, shard, jnp.zeros_like(shard)), axis)]
    ppermute x2, starting transfers between devices: 237 us -> 14.5 us  [extended(): lax.ppermute(lax.slice_in_dim(block, 0, width, axis=dim), axis, backward)]
    ppermute x40, waiting for transfers between devices: 238 us -> 294 us  [from_behind(): lax.ppermute(value, axis, [(source, source + steps) for source in range(i...]
    ppermute x40, starting transfers between devices: 155 us -> 179 us  [from_behind(): lax.ppermute(value, axis, [(source, source + steps) for source in range(i...]
  transfers between devices with their start and end apart: 44 -> 48, of which waited for: 35 -> 40; matrix products, arithmetic and copies ran while one was open for 2% -> 4% of each run, Pallas kernels for 0% -> 0%
where the time goes in v1:
time: 1260 us; the launch traced here: 1250 us
  waiting for transfers between devices  788 us (63%)
  starting transfers between devices  198 us (16%)
  matrix products  106 us (8%)
  local copies, waits for them, and re-layouts  90.8 us (7%)
  other arithmetic  55.6 us (4%)
  between operations  15.1 us (1%)
    all_gather x4, waiting for transfers between devices, from_root(): lax.all_gather(jnp.where(mine, shard, jnp.zeros_like(shard)), axis)  492 us
    ppermute x40, waiting for transfers between devices, from_behind(): lax.ppermute(value, axis, [(source, source + steps) for source in range(i...  294 us
    ppermute x40, starting transfers between devices, from_behind(): lax.ppermute(value, axis, [(source, source + steps) for source in range(i...  179 us
    dot_general x12, matrix products, doubling_maps(): jnp.einsum('bcl,cal->bal', current, moved, precision=highest)  106 us
    ppermute x12, local copies, waits for them, and re-layouts, from_behind(): lax.ppermute(value, axis, [(source, source + steps) for source in range(i...  39.4 us
    unnamed x26, other arithmetic  38 us
    select_n x10, local copies, waits for them, and re-layouts, doubling_maps(): jnp.where(exists, jnp.einsum('bcl,cal->bal', current, moved, precision=hi...  31 us
  transfers between devices with their start and end apart: 48, of which 40 were waited for; matrix products, arithmetic and copies ran while one was open for 4% of the time, Pallas kernels for 0%

profile of v1, /device:TPU:1, one launch (start us, length us, event | category | flops | bytes accessed | tf_op | source)
XLA Modules:
  0.0 1253.4 jit_solution(11771890342905836268)
XLA Ops:
  14.3 5.4 collective-permute-start.2
  26.1 17.9 %collective-permute-done = f32[48,128]{1,0:T(8,128)S(1)} collective-permute-done((f32[48,128]{1,0:T(8,128)S(1)}, f32[48,128]{1,0:T(8,128)S(1)}, u32[]{:S(2)}, u32[]{:S(2)}) %collective-permute-start) | collective-permute-done | bytes 24608 | tf_op jit(solution)/shard_map/ppermute | solution.py:12
  45.2 5.6 collective-permute-start.1
  55.1 7.0 multiply_reduce_fusion.26
  64.1 8.3 collective-permute-start.4
  72.5 5.2 collective-permute-start.3
  77.7 42.6 %collective-permute-done.3 = f32[48,128]{1,0:T(8,128)S(1)} collective-permute-done((f32[48,128]{1,0:T(8,128)S(1)}, f32[48,128]{1,0:T(8,128)S(1)}, u32[]{:S(2)}, u32[]{:S(2)}) %collective-permute-start.3) | collective-permute-done | bytes 24608 | tf_op jit(solution)/shard_map/ppermute | solution.py:12
  123.7 6.5 multiply_reduce_fusion.25
  133.4 9.1 collective-permute-start.6
  142.6 6.0 collective-permute-start.5
  149.6 17.3 %collective-permute-done.6 = f32[48,48,128]{2,1,0:T(8,128)} collective-permute-done((f32[48,48,128]{2,1,0:T(8,128)}, f32[48,48,128]{2,1,0:T(8,128)}, u32[]{:S(2)}, u32[]{:S(2)}) %collective-permute-start.6) | collective-permute-done | bytes 1179680 | tf_op jit(solution)/shard_map/ppermute | solution.py:12
  170.2 9.3 multiply_reduce_fusion.24
  182.8 38.2 %collective-permute-start.8 = (f32[48,48,128]{2,1,0:T(8,128)}, f32[48,48,128]{2,1,0:T(8,128)}, u32[]{:S(2)}, u32[]{:S(2)}) collective-permute-start(f32[48,48,128]{2,1,0:T(8,128)} %copy.30), channel_id=1, source_target_pairs={{0,32},{4,36},{8,40},{12,44},{16,48},{20,52},{24,56},{28,60},{32,6... | collective-permute-start | bytes 3538952 | tf_op jit(solution)/shard_map/ppermute | solution.py:12
  224.7 17.8 %collective-permute-done.8 = f32[48,48,128]{2,1,0:T(8,128)} collective-permute-done((f32[48,48,128]{2,1,0:T(8,128)}, f32[48,48,128]{2,1,0:T(8,128)}, u32[]{:S(2)}, u32[]{:S(2)}) %collective-permute-start.8) | collective-permute-done | bytes 1179680 | tf_op jit(solution)/shard_map/ppermute | solution.py:12
  245.7 9.4 multiply_reduce_fusion.23
  258.4 9.1 collective-permute-start.10
  271.2 17.0 %collective-permute-done.9 = f32[48,128]{1,0:T(8,128)S(1)} collective-permute-done((f32[48,128]{1,0:T(8,128)S(1)}, f32[48,128]{1,0:T(8,128)S(1)}, u32[]{:S(2)}, u32[]{:S(2)}) %collective-permute-start.9) | collective-permute-done | bytes 24608 | tf_op jit(solution)/shard_map/ppermute | solution.py:12
  291.6 9.3 multiply_reduce_fusion.22
  304.9 6.4 collective-permute-start.11
  324.7 5.7 collective-permute-done.11
  333.7 90.8 %all-gather.9.cloned.1.call-done = f32[3072,128]{1,0:T(8,128)} async-done(((f32[48,128]{1,0:T(8,128)}), f32[3072,128]{1,0:T(8,128)}) %all-gather.9.cloned.1.call-update) | async-done | bytes 1572880 | tf_op jit(solution)/shard_map/all_gather | solution.py:17
  426.2 9.3 multiply_reduce_fusion.21
  454.9 8.6 multiply_reduce_fusion.19
  469.5 9.3 collective-permute-done.16
  478.9 40.2 %collective-permute-done.17 = f32[48,48,128]{2,1,0:T(8,128)} collective-permute-done((f32[48,48,128]{2,1,0:T(8,128)}, f32[48,48,128]{2,1,0:T(8,128)}, u32[]{:S(2)}, u32[]{:S(2)}) %collective-permute-start.17) | collective-permute-done | bytes 1179680 | tf_op jit(solution)/shard_map/ppermute | solution.py:12
  522.3 9.3 multiply_reduce_fusion.18
  537.7 10.4 collective-permute-done.18
  548.2 14.5 %collective-permute-done.19 = f32[48,48,128]{2,1,0:T(8,128)} collective-permute-done((f32[48,48,128]{2,1,0:T(8,128)}, f32[48,48,128]{2,1,0:T(8,128)}, u32[]{:S(2)}, u32[]{:S(2)}) %collective-permute-start.19) | collective-permute-done | bytes 1179680 | tf_op jit(solution)/shard_map/ppermute | solution.py:12
  566.1 9.5 multiply_reduce_fusion.17
  581.5 17.0 %collective-permute-done.20 = f32[48,128]{1,0:T(8,128)S(1)} collective-permute-done((f32[48,128]{1,0:T(8,128)S(1)}, f32[48,128]{1,0:T(8,128)S(1)}, u32[]{:S(2)}, u32[]{:S(2)}) %collective-permute-start.20) | collective-permute-done | bytes 24608 | tf_op jit(solution)/shard_map/ppermute | solution.py:12
  601.9 9.4 multiply_reduce_fusion.16
  622.0 9.7 collective-permute-done.23
  635.0 9.5 multiply_reduce_fusion.15
  649.8 17.5 %collective-permute-done.24 = f32[48,48,128]{2,1,0:T(8,128)} collective-permute-done((f32[48,48,128]{2,1,0:T(8,128)}, f32[48,48,128]{2,1,0:T(8,128)}, u32[]{:S(2)}, u32[]{:S(2)}) %collective-permute-start.24) | collective-permute-done | bytes 1179680 | tf_op jit(solution)/shard_map/ppermute | solution.py:12
  670.5 158.0 %all-gather.11.cloned.1.call-done = f32[3072,128]{1,0:T(8,128)} async-done(((f32[48,128]{1,0:T(8,128)}), f32[3072,128]{1,0:T(8,128)}) %all-gather.11.cloned.1.call-update) | async-done | bytes 1572880 | tf_op jit(solution)/shard_map/all_gather | solution.py:17
  830.2 9.3 multiply_reduce_fusion.14
  846.4 7.3 collective-permute-start.27
  863.8 5.6 collective-permute-start.29
  871.3 8.6 collective-permute-start.30
  883.4 13.8 %collective-permute-start.31 = (f32[48,128]{1,0:T(8,128)S(1)}, f32[48,128]{1,0:T(8,128)S(1)}, u32[]{:S(2)}, u32[]{:S(2)}) collective-permute-start(f32[48,128]{1,0:T(8,128)S(1)} %bitcast_add_fusion.13), channel_id=1, source_target_pairs={{0,32},{4,36},{8,40},{12,44},{16,48},{20,52},{24,56},{28,60},{32,6... | collective-permute-start | bytes 73736 | tf_op jit(solution)/shard_map/ppermute | solution.py:12
  899.4 8.9 collective-permute-start.32
  911.9 5.1 collective-permute-start.33
  919.8 113.9 %all-gather.13.cloned.1.call-done = f32[3072,128]{1,0:T(8,128)} async-done(((f32[48,128]{1,0:T(8,128)}), f32[3072,128]{1,0:T(8,128)}) %all-gather.13.cloned.1.call-update) | async-done | bytes 1572880 | tf_op jit(solution)/shard_map/all_gather | solution.py:17
  1059.2 7.2 collective-permute-done.37
  1070.2 6.9 collective-permute-done.38
  1079.9 6.4 collective-permute-done.39
  1096.7 129.0 %all-gather.15.cloned.1.call-done = f32[3072,128]{1,0:T(8,128)} async-done(((f32[48,128]{1,0:T(8,128)}), f32[3072,128]{1,0:T(8,128)}) %all-gather.15.cloned.1.call-update) | async-done | bytes 1572880 | tf_op jit(solution)/shard_map/all_gather | solution.py:17
  1235.6 7.3 collective-permute-start.43
  (248 shorter events, 232.9 us)
Async XLA Ops:
  7.2 417.4 %all-gather.9.cloned.1.call-start = ((), (), s32[]{:S(2)}) async-start(), calls=%async_computation | async-start | bytes 1597440 | tf_op jit(solution)/shard_map/all_gather | solution.py:17
  14.3 37.5 %collective-permute-start.2 = (f32[48,48,128]{2,1,0:T(8,128)}, f32[48,48,128]{2,1,0:T(8,128)}, u32[]{:S(2)}, u32[]{:S(2)}) collective-permute-start(f32[48,48,128]{2,1,0:T(8,128)} %copy.22), channel_id=1, source_target_pairs={{0,4},{4,8},{8,12},{12,16},{16,20},{20,24},{24,28},{28,32},{32,36}... | collective-permute-start | bytes 3538952 | tf_op jit(solution)/shard_map/ppermute | solution.py:12
  23.5 20.5 %collective-permute-start = (f32[48,128]{1,0:T(8,128)S(1)}, f32[48,128]{1,0:T(8,128)S(1)}, u32[]{:S(2)}, u32[]{:S(2)}) collective-permute-start(f32[48,128]{1,0:T(8,128)S(1)} %subtract_bitcast_fusion.3), channel_id=1, source_target_pairs={{0,4},{4,8},{8,12},{12,16},{16,20},{20,24},{24,28},{28,32},{32,36}... | collective-permute-start | bytes 73736 | tf_op jit(solution)/shard_map/ppermute | solution.py:12
  45.2 6.5 collective-permute-start.1
  64.1 56.3 %collective-permute-start.4 = (f32[48,48,128]{2,1,0:T(8,128)}, f32[48,48,128]{2,1,0:T(8,128)}, u32[]{:S(2)}, u32[]{:S(2)}) collective-permute-start(f32[48,48,128]{2,1,0:T(8,128)} %copy.24), channel_id=1, source_target_pairs={{0,8},{4,12},{8,16},{12,20},{16,24},{20,28},{24,32},{28,36},{32,40... | collective-permute-start | bytes 3538952 | tf_op jit(solution)/shard_map/ppermute | solution.py:12
  72.5 47.8 %collective-permute-start.3 = (f32[48,128]{1,0:T(8,128)S(1)}, f32[48,128]{1,0:T(8,128)S(1)}, u32[]{:S(2)}, u32[]{:S(2)}) collective-permute-start(f32[48,128]{1,0:T(8,128)S(1)} %bitcast_add_fusion.29), channel_id=1, source_target_pairs={{0,16},{4,20},{8,24},{12,28},{16,32},{20,36},{24,40},{28,44},{32,4... | collective-permute-start | bytes 73736 | tf_op jit(solution)/shard_map/ppermute | solution.py:12
  133.4 33.5 %collective-permute-start.6 = (f32[48,48,128]{2,1,0:T(8,128)}, f32[48,48,128]{2,1,0:T(8,128)}, u32[]{:S(2)}, u32[]{:S(2)}) collective-permute-start(f32[48,48,128]{2,1,0:T(8,128)} %copy.27), channel_id=1, source_target_pairs={{0,16},{4,20},{8,24},{12,28},{16,32},{20,36},{24,40},{28,44},{32,4... | collective-permute-start | bytes 3538952 | tf_op jit(solution)/shard_map/ppermute | solution.py:12
  142.6 6.9 collective-permute-start.5
  182.8 59.7 %collective-permute-start.8 = (f32[48,48,128]{2,1,0:T(8,128)}, f32[48,48,128]{2,1,0:T(8,128)}, u32[]{:S(2)}, u32[]{:S(2)}) collective-permute-start(f32[48,48,128]{2,1,0:T(8,128)} %copy.30), channel_id=1, source_target_pairs={{0,32},{4,36},{8,40},{12,44},{16,48},{20,52},{24,56},{28,60},{32,6... | collective-permute-start | bytes 3538952 | tf_op jit(solution)/shard_map/ppermute | solution.py:12
  221.1 3.5 collective-permute-start.7
  258.4 29.9 %collective-permute-start.10 = (f32[48,48,128]{2,1,0:T(8,128)}, f32[48,48,128]{2,1,0:T(8,128)}, u32[]{:S(2)}, u32[]{:S(2)}) collective-permute-start(f32[48,48,128]{2,1,0:T(8,128)} %copy.33), channel_id=1, source_target_pairs={{0,64},{4,68},{8,72},{12,76},{16,80},{20,84},{24,88},{28,92},{32,9... | collective-permute-start | bytes 3538952 | tf_op jit(solution)/shard_map/ppermute | solution.py:12
  267.6 20.6 %collective-permute-start.9 = (f32[48,128]{1,0:T(8,128)S(1)}, f32[48,128]{1,0:T(8,128)S(1)}, u32[]{:S(2)}, u32[]{:S(2)}) collective-permute-start(f32[48,128]{1,0:T(8,128)S(1)} %bitcast_add_fusion.26), channel_id=1, source_target_pairs={{0,128},{4,132},{8,136},{12,140},{16,144},{20,148},{24,152},{28,15... | collective-permute-start | bytes 73736 | tf_op jit(solution)/shard_map/ppermute | solution.py:12
  301.6 526.9 %all-gather.11.cloned.1.call-start = ((), (), s32[]{:S(2)}) async-start(), calls=%async_computation.1 | async-start | bytes 1597440 | tf_op jit(solution)/shard_map/all_gather | solution.py:17
  304.9 25.5 %collective-permute-start.11 = (f32[48,48,128]{2,1,0:T(8,128)}, f32[48,48,128]{2,1,0:T(8,128)}, u32[]{:S(2)}, u32[]{:S(2)}) collective-permute-start(f32[48,48,128]{2,1,0:T(8,128)} %copy.36), channel_id=1, source_target_pairs={{0,128},{4,132},{8,136},{12,140},{16,144},{20,148},{24,152},{28,15... | collective-permute-start | bytes 3538952 | tf_op jit(solution)/shard_map/ppermute | solution.py:12
  320.4 130.4 %collective-permute-start.15 = (f32[48,48,128]{2,1,0:T(8,128)}, f32[48,48,128]{2,1,0:T(8,128)}, u32[]{:S(2)}, u32[]{:S(2)}) collective-permute-start(f32[48,48,128]{2,1,0:T(8,128)} %copy.40), channel_id=1, source_target_pairs={{4,0},{8,4},{12,8},{16,12},{20,16},{24,20},{28,24},{32,28},{36,32}... | collective-permute-start | bytes 3538952 | tf_op jit(solution)/shard_map/ppermute | solution.py:12
  435.6 4.5 collective-permute-start.12
  442.4 4.6 collective-permute-start.13
  449.3 5.5 collective-permute-start.14
  466.8 52.2 %collective-permute-start.17 = (f32[48,48,128]{2,1,0:T(8,128)}, f32[48,48,128]{2,1,0:T(8,128)}, u32[]{:S(2)}, u32[]{:S(2)}) collective-permute-start(f32[48,48,128]{2,1,0:T(8,128)} %copy.42), channel_id=1, source_target_pairs={{8,0},{12,4},{16,8},{20,12},{24,16},{28,20},{32,24},{36,28},{40,32... | collective-permute-start | bytes 3538952 | tf_op jit(solution)/shard_map/ppermute | solution.py:12
  468.2 10.6 collective-permute-start.16
  534.8 27.9 %collective-permute-start.19 = (f32[48,48,128]{2,1,0:T(8,128)}, f32[48,48,128]{2,1,0:T(8,128)}, u32[]{:S(2)}, u32[]{:S(2)}) collective-permute-start(f32[48,48,128]{2,1,0:T(8,128)} %copy.45), channel_id=1, source_target_pairs={{16,0},{20,4},{24,8},{28,12},{32,16},{36,20},{40,24},{44,28},{48,3... | collective-permute-start | bytes 3538952 | tf_op jit(solution)/shard_map/ppermute | solution.py:12
  536.2 12.0 collective-permute-start.18
  578.8 19.8 %collective-permute-start.21 = (f32[48,48,128]{2,1,0:T(8,128)}, f32[48,48,128]{2,1,0:T(8,128)}, u32[]{:S(2)}, u32[]{:S(2)}) collective-permute-start(f32[48,48,128]{2,1,0:T(8,128)} %copy.48), channel_id=1, source_target_pairs={{32,0},{36,4},{40,8},{44,12},{48,16},{52,20},{56,24},{60,28},{64,3... | collective-permute-start | bytes 3538952 | tf_op jit(solution)/shard_map/ppermute | solution.py:12
  580.2 18.3 %collective-permute-start.20 = (f32[48,128]{1,0:T(8,128)S(1)}, f32[48,128]{1,0:T(8,128)S(1)}, u32[]{:S(2)}, u32[]{:S(2)}) collective-permute-start(f32[48,128]{1,0:T(8,128)S(1)} %bitcast_add_fusion.20), channel_id=1, source_target_pairs={{64,0},{68,4},{72,8},{76,12},{80,16},{84,20},{88,24},{92,28},{96,3... | collective-permute-start | bytes 73736 | tf_op jit(solution)/shard_map/ppermute | solution.py:12
  614.5 17.3 %collective-permute-start.23 = (f32[48,48,128]{2,1,0:T(8,128)}, f32[48,48,128]{2,1,0:T(8,128)}, u32[]{:S(2)}, u32[]{:S(2)}) collective-permute-start(f32[48,48,128]{2,1,0:T(8,128)} %copy.51), channel_id=1, source_target_pairs={{64,0},{68,4},{72,8},{76,12},{80,16},{84,20},{88,24},{92,28},{96,3... | collective-permute-start | bytes 3538952 | tf_op jit(solution)/shard_map/ppermute | solution.py:12
  615.9 6.1 collective-permute-start.22
  645.2 388.5 %all-gather.13.cloned.1.call-start = ((), (), s32[]{:S(2)}) async-start(), calls=%async_computation.2 | async-start | bytes 1597440 | tf_op jit(solution)/shard_map/all_gather | solution.py:17
  648.5 18.8 %collective-permute-start.24 = (f32[48,48,128]{2,1,0:T(8,128)}, f32[48,48,128]{2,1,0:T(8,128)}, u32[]{:S(2)}, u32[]{:S(2)}) collective-permute-start(f32[48,48,128]{2,1,0:T(8,128)} %copy.54), channel_id=1, source_target_pairs={{128,0},{132,4},{136,8},{140,12},{144,16},{148,20},{152,24},{156,2... | collective-permute-start | bytes 3538952 | tf_op jit(solution)/shard_map/ppermute | solution.py:12
  839.5 4.6 collective-permute-start.25
  846.4 9.4 collective-permute-start.27
  853.7 3.1 collective-permute-start.26
  858.0 3.4 collective-permute-start.28
  863.8 6.3 collective-permute-start.29
  871.3 9.6 collective-permute-start.30
  883.4 14.8 %collective-permute-start.31 = (f32[48,128]{1,0:T(8,128)S(1)}, f32[48,128]{1,0:T(8,128)S(1)}, u32[]{:S(2)}, u32[]{:S(2)}) collective-permute-start(f32[48,128]{1,0:T(8,128)S(1)} %bitcast_add_fusion.13), channel_id=1, source_target_pairs={{0,32},{4,36},{8,40},{12,44},{16,48},{20,52},{24,56},{28,60},{32,6... | collective-permute-start | bytes 73736 | tf_op jit(solution)/shard_map/ppermute | solution.py:12
  899.4 9.8 collective-permute-start.32
  911.9 6.1 collective-permute-start.33
  919.7 306.0 %all-gather.15.cloned.1.call-start = ((), (), s32[]{:S(2)}) async-start(), calls=%async_computation.3 | async-start | bytes 1597440 | tf_op jit(solution)/shard_map/all_gather | solution.py:17
  1038.0 3.3 collective-permute-start.34
  1043.6 4.8 collective-permute-start.35
  1050.8 5.6 collective-permute-start.36
  1057.6 8.7 collective-permute-start.37
  1068.9 8.2 collective-permute-start.38
  1078.3 7.9 collective-permute-start.39
  1088.8 6.1 collective-permute-start.40
  1229.9 4.6 collective-permute-start.41
  1235.6 9.4 collective-permute-start.43
  1242.9 3.1 collective-permute-start.42
  (10 other events, 345.2 us)
Sparse Core Ops, SparseCore 0:
  301.7 122.7 all-gather.8
  645.3 183.1 all-gather.10
  919.9 113.8 all-gather.12
  1096.9 128.8 all-gather.14
